TPU v7x, 128 devices: a whole 4x4x4 slice. The times are simulated.
128 devices in a mesh: row: 8 (over y, core), col: 16 (over x, z).
Axes of the slice: x: 4, y: 4, z: 4, core: 2. Of those that a mesh axis runs over, the one named last changes fastest.
Arguments:
- probes: bfloat16 [4, 32768, 256], P(None, ('row', 'col')), may hold values from -6 to 6
- points: bfloat16 [16, 4, 32768], P(None, None, ('row', 'col')), may hold values from -8 to 8
- leaf_skeleton: int32 [256, 64], P(('row', 'col')), may hold values from 0 to 127, as said below
- skeleton_one: int32 [128, 64], P(('row', 'col')), may hold values from 0 to 127, as said below
- skeleton_two: int32 [64, 64], P('row'), may hold values from 0 to 127, as said below
- skeleton_three: int32 [32, 64], P('row'), may hold values from 0 to 127, as said below
Outputs:
- leaf_interp: float32 [256, 128, 64], P(('row', 'col'))
- upper_interp: float32 [3, 128, 128, 64], P(None, ('row', 'col'))
- top_state: float32 [2, 128, 64, 256], P(None, ('row', 'col'))
Inputs may be any that keep to these rules, and one draw needn't show every extreme that they name: `leaf_skeleton`: each row names 64 different rows of its leaf, in ascending order. `skeleton_one`: each row names 64 different rows of the node's stacked child skeletons, in ascending order. `skeleton_two`: each row names 64 different rows of the node's stacked child skeletons, in ascending order. `skeleton_three`: each row names 64 different rows of the node's stacked child skeletons, in ascending order.
All inputs are finite; a program needn't handle non-finite values.
Results may differ from a plain program's by a relative error of at most 0.0059.
Values may be sent and summed in bfloat16 or wider, within the bound.
A program may use at most 64 MiB of HBM per device.

v0:
```python
from functools import partial
import math
import jax
import jax.numpy as jnp
from jax import lax
from jax.sharding import PartitionSpec as P

LEAF = 128
exact_mode = lax.Precision.HIGHEST


def swapped(value, axis, bit):
    return lax.ppermute(value, axis, [(i, i ^ 1 << bit) for i in range(lax.axis_size(axis))])


def couple(row_feats, col_feats, kernel_gain):
    cross = jnp.dot(row_feats.T, col_feats, precision=exact_mode)
    row_sq = jnp.sum(row_feats * row_feats, axis=0)
    col_sq = jnp.sum(col_feats * col_feats, axis=0)
    feat_count = row_feats.shape[0]
    return kernel_gain * jnp.exp(
        (2.0 * cross - row_sq[:, None] - col_sq[None, :]) / (2.0 * feat_count)
    )


def interpolate(stacked, chosen):
    skeleton = jnp.take(stacked, chosen, axis=0)
    gram_mat = jnp.dot(skeleton, skeleton.T, precision=exact_mode)
    damping = 0.05 * jnp.sum(skeleton * skeleton) / chosen.shape[0] + 1e-05
    factor = jnp.linalg.cholesky(gram_mat + damping * jnp.eye(chosen.shape[0], dtype=stacked.dtype))
    cross_mat = jnp.dot(stacked, skeleton.T, precision=exact_mode)
    solved = jax.scipy.linalg.cho_solve((factor, True), cross_mat.T)
    return (solved.T, skeleton)


def leaf_level(leaf_rows, leaf_probes, coords, chosen):
    interp, skeleton = interpolate(leaf_rows, chosen)
    reduced = jnp.dot(interp.T, leaf_probes.astype(interp.dtype), precision=exact_mode)
    picked = jnp.take(coords, chosen, axis=1).astype(jnp.float32)
    return (interp, (skeleton, reduced, picked))


def merge_pair(first_child, second_child, chosen, kernel_gain):
    first_samples, first_reduced, first_points = first_child
    second_samples, second_reduced, second_points = second_child
    upper_rows = first_samples - jnp.dot(
        couple(first_points, second_points, kernel_gain), second_reduced, precision=exact_mode
    )
    lower_rows = second_samples - jnp.dot(
        couple(second_points, first_points, kernel_gain), first_reduced, precision=exact_mode
    )
    stacked = jnp.concatenate([upper_rows, lower_rows], axis=0)
    interp, skeleton = interpolate(stacked, chosen)
    reduced = jnp.dot(
        interp.T, jnp.concatenate([first_reduced, second_reduced], axis=0), precision=exact_mode
    )
    joined = jnp.take(jnp.concatenate([first_points, second_points], axis=1), chosen, axis=1)
    return (interp, (skeleton, reduced, joined))


def take_first(values):
    return values[0]


def take_second(values):
    return values[1]


def local(probes, points, leaf_skeleton, skeleton_one, skeleton_two, skeleton_three):
    feat_count = points.shape[0]
    own_rows = probes.shape[1]
    row_count = lax.axis_size("row")
    col_count = lax.axis_size("col")
    row_pos = lax.axis_index("row")
    col_pos = lax.axis_index("col")
    row_span = own_rows * col_count
    extent = row_span * row_count
    kernel_gain = 16.0 / math.sqrt(4 * extent)
    probe_cols = lax.all_gather(probes, "row", axis=1, tiled=True).reshape(
        4 * row_count * own_rows, -1
    )
    row_coords = lax.all_gather(points[:, 0], "col", axis=1, tiled=True)
    col_coords = lax.all_gather(points, "row", axis=2, tiled=True).reshape(
        feat_count, 4 * row_count * own_rows
    )
    col_wide = col_coords.astype(jnp.float32)
    col_sq = jnp.sum(col_wide * col_wide, axis=0)
    row_leaf = (row_pos * row_span + jnp.arange(row_span, dtype=jnp.int32)) // LEAF
    quarter_len = row_count * own_rows
    offsets = jnp.arange(4 * quarter_len, dtype=jnp.int32)
    quarter = offsets // quarter_len
    within = offsets % quarter_len
    col_leaf = (
        quarter * extent + within // own_rows * row_span + col_pos * own_rows + within % own_rows
    ) // LEAF
    height = 512

    def one_block(first_row):
        coords = lax.dynamic_slice_in_dim(row_coords, first_row, height, 1)
        leaves = lax.dynamic_slice_in_dim(row_leaf, first_row, height, 0)
        cross = lax.dot_general(
            coords, col_coords, (((0,), (0,)), ((), ())), preferred_element_type=jnp.float32
        )
        row_wide = coords.astype(jnp.float32)
        row_sq = jnp.sum(row_wide * row_wide, axis=0)
        kernel_tile = kernel_gain * jnp.exp(
            (2.0 * cross - row_sq[:, None] - col_sq[None, :]) / (2.0 * feat_count)
        )
        kernel_tile = jnp.where(leaves[:, None] == col_leaf[None, :], 0.0, kernel_tile).astype(
            jnp.bfloat16
        )
        return jnp.dot(kernel_tile, probe_cols, preferred_element_type=jnp.float32)

    starts = jnp.arange(row_span // height, dtype=jnp.int32) * height
    summed = lax.psum(lax.map(one_block, starts).reshape(row_span, -1), "col")
    owned = lax.dynamic_slice_in_dim(summed, col_pos * own_rows, own_rows, 0)
    leaf_count = own_rows // LEAF
    leaf_rows = owned.reshape(leaf_count, LEAF, -1)
    leaf_probes = probes[0].reshape(leaf_count, LEAF, -1)
    leaf_coords = points[:, 0].reshape(feat_count, leaf_count, LEAF).transpose(1, 0, 2)
    leaf_interp, carried = jax.vmap(leaf_level)(leaf_rows, leaf_probes, leaf_coords, leaf_skeleton)
    first_child = jax.tree.map(take_first, carried)
    second_child = jax.tree.map(take_second, carried)
    interp_one, carried = merge_pair(first_child, second_child, skeleton_one[0], kernel_gain)
    upper_list = [interp_one]
    for bit_num in range(2):
        partner = swapped((carried[0], carried[1], carried[2]), "col", bit_num)
        mine_first = col_pos >> bit_num & 1 == 0
        first_child = jax.tree.map(partial(jnp.where, mine_first), carried, partner)
        second_child = jax.tree.map(partial(jnp.where, mine_first), partner, carried)
        table_rows = skeleton_two if bit_num == 0 else skeleton_three
        chosen = lax.dynamic_index_in_dim(table_rows, col_pos // (2 << bit_num), 0, keepdims=False)
        interp_up, carried = merge_pair(first_child, second_child, chosen, kernel_gain)
        upper_list.append(interp_up)
    upper_interp = jnp.stack(upper_list)[:, None]
    top_state = jnp.stack([carried[0], carried[1]])[:, None]
    return (leaf_interp, upper_interp, top_state)


def solution(mesh):
    placed = (
        P(None, ("row", "col"), None),
        P(None, None, ("row", "col")),
        P(("row", "col"), None),
        P(("row", "col"), None),
        P("row", None),
        P("row", None),
    )
    return jax.shard_map(
        local,
        mesh=mesh,
        in_specs=placed,
        out_specs=(
            P(("row", "col"), None, None),
            P(None, ("row", "col"), None, None),
            P(None, ("row", "col"), None, None),
        ),
        check_vma=False,
    )
```

profile of v0, /device:TPU:0, one launch (start us, length us, event | category | flops | bytes accessed | tf_op | source)
XLA Modules:
  0.0 333.6 jit_solution(17776641699340166567)
XLA Ops:
  8.7 12.7 %all_gather.10 = bf16[16,4,2048]{2,1,0:T(4,128)(2,1)S(1)} all-gather(bf16[16,4,256]{2,1,0:T(4,128)(2,1)} %param.16), channel_id=1, replica_groups=mesh['row'=8,'col'=16] {'row'}, dimensions={2}, use_global_device_ids=true | all-gather | bytes 294912 | tf_op jit(solution)/shard_map/all_gather | solution.py:83
  21.8 25.1 %all-gather = bf16[16,1,4096]{2,0,1:T(8,128)(2,1)S(1)} all-gather(bf16[16,1,256]{2,0,1:T(8,128)(2,1)S(1)} %copy.60), channel_id=2, replica_groups=mesh['row'=8,'col'=16] {'col'}, dimensions={2}, use_global_device_ids=true | all-gather | bytes 139264 | tf_op jit(solution)/shard_map/all_gather | solution.py:82
  46.9 88.3 %while.11 = (s32[]{:T(128)}, f32[8,512,256]{2,1,0:T(8,128)}, s32[8]{0:T(128)S(1)}, s32[4096]{0:T(1024)S(1)}, bf16[16,4096]{1,0:T(8,128)(2,1)S(1)}, /*index=5*/bf...) while((s32[]{:T(128)}, f32[8,512,256]{2,1,0:T(8,128)}, ...), condition=%wide.region_3.4_spmd.clone, body=%wide.region_1.3_spmd.clone.sunk | while | flops 2315697664 | bytes 5122239 | solution.py:115
  49.7 8.3 %fusion.176 = f32[8,512,256]{2,1,0:T(8,128)} fusion(f32[8,512,256]{2,1,0:T(8,128)} %get-tuple-element.213, s32[]{:T(128)S(6)} %copy.67, bf16[8192,256]{1,0:T(8,128)(2,1)} %get-tuple-element.231, bf16[16,8192]{1,0:T(8,128)(2,1)S(1)} %get-tuple-element.229, f32[8192]{0:T(1024)S(1)} %get-tuple-element.230, f32[512]{0:T(512)S(1)} %multiply_reduce_fusion.13, ...), kind=kOutput, calls=%fused_computation.11.clone.1 | convolution fusion | flops 2315255808 | bytes 5066760 | tf_op jit(solution)/shard_map/while/body/eval_jaxpr/dot_general | solution.py:112
  60.7 8.3 %fusion.176 = f32[8,512,256]{2,1,0:T(8,128)} fusion(f32[8,512,256]{2,1,0:T(8,128)} %get-tuple-element.213, s32[]{:T(128)S(6)} %copy.67, bf16[8192,256]{1,0:T(8,128)(2,1)} %get-tuple-element.231, bf16[16,8192]{1,0:T(8,128)(2,1)S(1)} %get-tuple-element.229, f32[8192]{0:T(1024)S(1)} %get-tuple-element.230, f32[512]{0:T(512)S(1)} %multiply_reduce_fusion.13, ...), kind=kOutput, calls=%fused_computation.11.clone.1 | convolution fusion | flops 2315255808 | bytes 5066760 | tf_op jit(solution)/shard_map/while/body/eval_jaxpr/dot_general | solution.py:112
  71.8 8.3 %fusion.176 = f32[8,512,256]{2,1,0:T(8,128)} fusion(f32[8,512,256]{2,1,0:T(8,128)} %get-tuple-element.213, s32[]{:T(128)S(6)} %copy.67, bf16[8192,256]{1,0:T(8,128)(2,1)} %get-tuple-element.231, bf16[16,8192]{1,0:T(8,128)(2,1)S(1)} %get-tuple-element.229, f32[8192]{0:T(1024)S(1)} %get-tuple-element.230, f32[512]{0:T(512)S(1)} %multiply_reduce_fusion.13, ...), kind=kOutput, calls=%fused_computation.11.clone.1 | convolution fusion | flops 2315255808 | bytes 5066760 | tf_op jit(solution)/shard_map/while/body/eval_jaxpr/dot_general | solution.py:112
  82.8 8.3 %fusion.176 = f32[8,512,256]{2,1,0:T(8,128)} fusion(f32[8,512,256]{2,1,0:T(8,128)} %get-tuple-element.213, s32[]{:T(128)S(6)} %copy.67, bf16[8192,256]{1,0:T(8,128)(2,1)} %get-tuple-element.231, bf16[16,8192]{1,0:T(8,128)(2,1)S(1)} %get-tuple-element.229, f32[8192]{0:T(1024)S(1)} %get-tuple-element.230, f32[512]{0:T(512)S(1)} %multiply_reduce_fusion.13, ...), kind=kOutput, calls=%fused_computation.11.clone.1 | convolution fusion | flops 2315255808 | bytes 5066760 | tf_op jit(solution)/shard_map/while/body/eval_jaxpr/dot_general | solution.py:112
  93.9 8.3 %fusion.176 = f32[8,512,256]{2,1,0:T(8,128)} fusion(f32[8,512,256]{2,1,0:T(8,128)} %get-tuple-element.213, s32[]{:T(128)S(6)} %copy.67, bf16[8192,256]{1,0:T(8,128)(2,1)} %get-tuple-element.231, bf16[16,8192]{1,0:T(8,128)(2,1)S(1)} %get-tuple-element.229, f32[8192]{0:T(1024)S(1)} %get-tuple-element.230, f32[512]{0:T(512)S(1)} %multiply_reduce_fusion.13, ...), kind=kOutput, calls=%fused_computation.11.clone.1 | convolution fusion | flops 2315255808 | bytes 5066760 | tf_op jit(solution)/shard_map/while/body/eval_jaxpr/dot_general | solution.py:112
  104.9 8.3 %fusion.176 = f32[8,512,256]{2,1,0:T(8,128)} fusion(f32[8,512,256]{2,1,0:T(8,128)} %get-tuple-element.213, s32[]{:T(128)S(6)} %copy.67, bf16[8192,256]{1,0:T(8,128)(2,1)} %get-tuple-element.231, bf16[16,8192]{1,0:T(8,128)(2,1)S(1)} %get-tuple-element.229, f32[8192]{0:T(1024)S(1)} %get-tuple-element.230, f32[512]{0:T(512)S(1)} %multiply_reduce_fusion.13, ...), kind=kOutput, calls=%fused_computation.11.clone.1 | convolution fusion | flops 2315255808 | bytes 5066760 | tf_op jit(solution)/shard_map/while/body/eval_jaxpr/dot_general | solution.py:112
  116.0 8.3 %fusion.176 = f32[8,512,256]{2,1,0:T(8,128)} fusion(f32[8,512,256]{2,1,0:T(8,128)} %get-tuple-element.213, s32[]{:T(128)S(6)} %copy.67, bf16[8192,256]{1,0:T(8,128)(2,1)} %get-tuple-element.231, bf16[16,8192]{1,0:T(8,128)(2,1)S(1)} %get-tuple-element.229, f32[8192]{0:T(1024)S(1)} %get-tuple-element.230, f32[512]{0:T(512)S(1)} %multiply_reduce_fusion.13, ...), kind=kOutput, calls=%fused_computation.11.clone.1 | convolution fusion | flops 2315255808 | bytes 5066760 | tf_op jit(solution)/shard_map/while/body/eval_jaxpr/dot_general | solution.py:112
  127.0 8.3 %fusion.176 = f32[8,512,256]{2,1,0:T(8,128)} fusion(f32[8,512,256]{2,1,0:T(8,128)} %get-tuple-element.213, s32[]{:T(128)S(6)} %copy.67, bf16[8192,256]{1,0:T(8,128)(2,1)} %get-tuple-element.231, bf16[16,8192]{1,0:T(8,128)(2,1)S(1)} %get-tuple-element.229, f32[8192]{0:T(1024)S(1)} %get-tuple-element.230, f32[512]{0:T(512)S(1)} %multiply_reduce_fusion.13, ...), kind=kOutput, calls=%fused_computation.11.clone.1 | convolution fusion | flops 2315255808 | bytes 5066760 | tf_op jit(solution)/shard_map/while/body/eval_jaxpr/dot_general | solution.py:112
  146.1 3.6 %collective-permute-done.4 = f32[16,64]{0,1:T(8,128)S(1)} collective-permute-done((f32[16,64]{0,1:T(8,128)S(1)}, f32[16,64]{0,1:T(8,128)S(1)}, u32[]{:S(2)}, u32[]{:S(2)}) %collective-permute-start.4) | collective-permute-done | bytes 4128 | tf_op jit(solution)/shard_map/ppermute | solution.py:13
  149.8 87.9 %all-reduce.2.cloned.1.call-done = f32[4096,256]{1,0:T(8,128)} async-done(((f32[4096,256]{1,0:T(8,128)}), f32[4096,256]{1,0:T(8,128)}) %all-reduce.2.cloned.1.call-update) | async-done | bytes 4194320 | tf_op jit(solution)/shard_map/psum | solution.py:115
  241.0 11.7 %custom-call.18 = f32[2,64,64]{2,1,0:T(8,128)S(1)} custom-call(f32[2,64,64]{2,1,0:T(8,128)S(1)} %fusion.80), custom_call_target="Cholesky" | custom-call | tf_op jit(solution)/shard_map/vmap(jit(cholesky))/cholesky | solution.py:30
  253.0 9.8 %custom-call.19 = f32[2,1,64,64]{2,3,1,0:T(8,128)S(1)} custom-call(f32[2,1,64,64]{3,2,1,0:T(8,128)S(1)} %select_bitcast_fusion), custom_call_target="InvertDiagBlocksLowerTriangular" | custom-call | tf_op jit(solution)/shard_map/vmap(jit(_cho_solve))/triangular_solve | solution.py:32
  266.6 5.8 %cholesky.106 = f32[64,64]{1,0:T(8,128)S(1)} custom-call(f32[64,64]{1,0:T(8,128)S(1)} %fusion.101), custom_call_target="Cholesky" | custom-call | tf_op jit(solution)/shard_map/jit(cholesky)/cholesky | solution.py:30
  273.8 4.9 %custom-call.26 = f32[1,64,64]{1,2,0:T(8,128)S(1)} custom-call(f32[1,64,64]{2,1,0:T(8,128)S(1)} %fusion.84), custom_call_target="InvertDiagBlocksLowerTriangular" | custom-call | tf_op jit(solution)/shard_map/jit(_cho_solve)/triangular_solve | solution.py:32
  281.7 2.5 collective-permute-done.2
  287.9 5.8 %cholesky.117 = f32[64,64]{1,0:T(8,128)S(1)} custom-call(f32[64,64]{1,0:T(8,128)S(1)} %fusion.96), custom_call_target="Cholesky" | custom-call | tf_op jit(solution)/shard_map/jit(cholesky)/cholesky | solution.py:30
  295.1 4.9 %custom-call.27 = f32[1,64,64]{1,2,0:T(8,128)S(1)} custom-call(f32[1,64,64]{2,1,0:T(8,128)S(1)} %fusion.85), custom_call_target="InvertDiagBlocksLowerTriangular" | custom-call | tf_op jit(solution)/shard_map/jit(_cho_solve)/triangular_solve | solution.py:32
  300.6 2.9 collective-permute-start.5
  306.7 3.1 collective-permute-done.3
  312.7 5.8 %cholesky.128 = f32[64,64]{1,0:T(8,128)S(1)} custom-call(f32[64,64]{1,0:T(8,128)S(1)} %fusion.91), custom_call_target="Cholesky" | custom-call | tf_op jit(solution)/shard_map/jit(cholesky)/cholesky | solution.py:30
  319.9 4.9 %custom-call.28 = f32[1,64,64]{1,2,0:T(8,128)S(1)} custom-call(f32[1,64,64]{2,1,0:T(8,128)S(1)} %fusion.86), custom_call_target="InvertDiagBlocksLowerTriangular" | custom-call | tf_op jit(solution)/shard_map/jit(_cho_solve)/triangular_solve | solution.py:32
  (160 shorter events, 43.4 us)
Async XLA Ops:
  7.2 39.8 %all-gather.3.cloned.1.call-start = ((), (), s32[]{:S(2)}) async-start(), calls=%async_computation | async-start | bytes 4718592 | tf_op jit(solution)/shard_map/all_gather | solution.py:79
  7.9 229.8 %all-reduce.2.cloned.1.call-start = ((), (), s32[]{:S(2)}) async-start(), calls=%async_computation.1 | async-start | bytes 8388608 | tf_op jit(solution)/shard_map/psum | solution.py:115
  135.3 0.7 copy-start.1
  135.3 2.3 copy-start.2
  138.3 4.0 %collective-permute-start.1 = (f32[16,64]{0,1:T(8,128)S(1)}, f32[16,64]{0,1:T(8,128)S(1)}, u32[]{:S(2)}, u32[]{:S(2)}) collective-permute-start(f32[16,64]{0,1:T(8,128)S(1)} %select_bitcast_fusion.3), channel_id=1, source_target_pairs={{0,1},{1,0},{2,3},{3,2},{4,5},{5,4},{6,7},{7,6},{8,9},{9,8},{10,11... | collective-permute-start | bytes 12296 | tf_op jit(solution)/shard_map/ppermute | solution.py:13
  143.1 6.5 %collective-permute-start.4 = (f32[16,64]{0,1:T(8,128)S(1)}, f32[16,64]{0,1:T(8,128)S(1)}, u32[]{:S(2)}, u32[]{:S(2)}) collective-permute-start(f32[16,64]{0,1:T(8,128)S(1)} %select_bitcast_fusion.2), channel_id=1, source_target_pairs={{0,2},{1,3},{2,0},{3,1},{4,6},{5,7},{6,4},{7,5},{8,10},{9,11},{10,... | collective-permute-start | bytes 12296 | tf_op jit(solution)/shard_map/ppermute | solution.py:13
  263.3 49.3 %copy-start = (f32[2,64,128]{2,1,0:T(8,128)}, f32[2,64,128]{2,1,0:T(8,128)S(1)}, u32[]{:S(2)}) copy-start(f32[2,64,128]{2,1,0:T(8,128)S(1)} %fusion.75) | copy-start | bytes 196612
  279.3 4.9 %collective-permute-start.2 = (f32[64,256]{1,0:T(8,128)S(1)}, f32[64,256]{1,0:T(8,128)S(1)}, u32[]{:S(2)}, u32[]{:S(2)}) collective-permute-start(f32[64,256]{1,0:T(8,128)S(1)} %fusion.64), channel_id=1, source_target_pairs={{0,1},{1,0},{2,3},{3,2},{4,5},{5,4},{6,7},{7,6},{8,9},{9,8},{10,11... | collective-permute-start | bytes 196616 | tf_op jit(solution)/shard_map/ppermute | solution.py:13
  280.8 4.3 %collective-permute-start = (f32[64,256]{1,0:T(8,128)S(1)}, f32[64,256]{1,0:T(8,128)S(1)}, u32[]{:S(2)}, u32[]{:S(2)}) collective-permute-start(f32[64,256]{1,0:T(8,128)S(1)} %get-tuple-element.110), channel_id=1, source_target_pairs={{0,1},{1,0},{2,3},{3,2},{4,5},{5,4},{6,7},{7,6},{8,9},{9,8},{10,11... | collective-permute-start | bytes 196616 | tf_op jit(solution)/shard_map/ppermute | solution.py:13
  300.6 5.8 %collective-permute-start.5 = (f32[64,256]{1,0:T(8,128)S(1)}, f32[64,256]{1,0:T(8,128)S(1)}, u32[]{:S(2)}, u32[]{:S(2)}) collective-permute-start(f32[64,256]{1,0:T(8,128)S(1)} %fusion.68), channel_id=1, source_target_pairs={{0,2},{1,3},{2,0},{3,1},{4,6},{5,7},{6,4},{7,5},{8,10},{9,11},{10,... | collective-permute-start | bytes 196616 | tf_op jit(solution)/shard_map/ppermute | solution.py:13
  303.8 6.1 %collective-permute-start.3 = (f32[64,256]{1,0:T(8,128)S(1)}, f32[64,256]{1,0:T(8,128)S(1)}, u32[]{:S(2)}, u32[]{:S(2)}) collective-permute-start(f32[64,256]{1,0:T(8,128)S(1)} %get-tuple-element.108), channel_id=1, source_target_pairs={{0,2},{1,3},{2,0},{3,1},{4,6},{5,7},{6,4},{7,5},{8,10},{9,11},{10,... | collective-permute-start | bytes 196616 | tf_op jit(solution)/shard_map/ppermute | solution.py:13
Sparse Core Ops, SparseCore 0:
  9.7 34.5 all-gather.2
  135.4 102.2 all-reduce.1
where the time goes:
time: 334 us
  waiting for transfers between devices  101 us (30%)
  matrix products  73.3 us (22%)
  other arithmetic  64.5 us (19%)
  blocking collectives  37.8 us (11%)
  between operations  16.6 us (5%)
  loops' own time  15.6 us (5%)
  local copies, waits for them, and re-layouts  15.3 us (5%)
  starting transfers between devices  9.94 us (3%)
    psum x1, waiting for transfers between devices, local(): summed = lax.psum(lax.map(one_block, starts).reshape(row_span, -1), 'col')  87.9 us
    dot_general x8, matrix products, one_block(): return jnp.dot(kernel_tile, probe_cols, preferred_element_type=jnp.float32)  66.3 us
    another operation x13, other arithmetic, interpolate(): jnp.linalg.cholesky(gram_mat + damping * jnp.eye(chosen.shape[0], dtype=s...  31.4 us
    another operation x9, other arithmetic, interpolate(): solved = jax.scipy.linalg.cho_solve((factor, True), cross_mat.T)  26.6 us
    all_gather x1, blocking collectives, local(): row_coords = lax.all_gather(points[:, 0], 'col', axis=1, tiled=True)  25.1 us
    another operation x1, loops' own time, local(): summed = lax.psum(lax.map(one_block, starts).reshape(row_span, -1), 'col')  15.6 us
    all_gather x1, blocking collectives, local(): lax.all_gather(points, 'row', axis=2, tiled=True)  12.7 us
    ppermute x6, waiting for transfers between devices, swapped(): lax.ppermute(value, axis, [(i, i ^ 1 << bit) for i in range(lax.axis_size...  12 us
  transfers between devices with their start and end apart: 8, of which 7 were waited for; matrix products, arithmetic and copies ran while one was open for 2% of the time, Pallas kernels for 0%

commit v1 on v0

--- a/solution.py
+++ b/solution.py
@@ -7,6 +7,11 @@
 
 LEAF = 128
 exact_mode = lax.Precision.HIGHEST
+
+
+def all_parts(value, axis, dim):
+    shards = lax.all_gather(value, axis)
+    return jnp.concatenate(shards, axis=dim)
 
 
 def swapped(value, axis, bit):
@@ -79,7 +84,7 @@
     probe_cols = lax.all_gather(probes, "row", axis=1, tiled=True).reshape(
         4 * row_count * own_rows, -1
     )
-    row_coords = lax.all_gather(points[:, 0], "col", axis=1, tiled=True)
+    row_coords = all_parts(points[:, 0], "col", 1)
     col_coords = lax.all_gather(points, "row", axis=2, tiled=True).reshape(
         feat_count, 4 * row_count * own_rows
     )

time: 334 us -> 336 us (level)
  no operation moved by 1% of the time
where the time goes in v1:
time: 336 us; the launch traced here: 335 us
  waiting for transfers between devices  101 us (30%)
  matrix products  73.3 us (22%)
  other arithmetic  64.5 us (19%)
  blocking collectives  38.8 us (12%)
  between operations  16.6 us (5%)
  loops' own time  15.6 us (5%)
  local copies, waits for them, and re-layouts  15.3 us (5%)
  starting transfers between devices  10.3 us (3%)
    psum x1, waiting for transfers between devices, local(): summed = lax.psum(lax.map(one_block, starts).reshape(row_span, -1), 'col')  88.6 us
    dot_general x8, matrix products, one_block(): return jnp.dot(kernel_tile, probe_cols, preferred_element_type=jnp.float32)  66.3 us
    another operation x13, other arithmetic, interpolate(): jnp.linalg.cholesky(gram_mat + damping * jnp.eye(chosen.shape[0], dtype=s...  31.4 us
    another operation x9, other arithmetic, interpolate(): solved = jax.scipy.linalg.cho_solve((factor, True), cross_mat.T)  26.6 us
    all_gather x1, blocking collectives, all_parts(): shards = lax.all_gather(value, axis)  25.2 us
    another operation x1, loops' own time, local(): summed = lax.psum(lax.map(one_block, starts).reshape(row_span, -1), 'col')  15.6 us
    all_gather x1, blocking collectives, local(): lax.all_gather(points, 'row', axis=2, tiled=True)  13.7 us
    ppermute x6, waiting for transfers between devices, swapped(): lax.ppermute(value, axis, [(i, i ^ 1 << bit) for i in range(lax.axis_size...  11.5 us
  transfers between devices with their start and end apart: 8, of which 7 were waited for; matrix products, arithmetic and copies ran while one was open for 2% of the time, Pallas kernels for 0%

profile of v1, /device:TPU:0, one launch (start us, length us, event | category | flops | bytes accessed | tf_op | source)
XLA Modules:
  0.0 335.2 jit_solution(2079729645228889725)
XLA Ops:
  8.7 25.2 %all-gather = bf16[256,1,256]{2,0,1:T(8,128)(2,1)S(1)} all-gather(bf16[16,1,256]{2,0,1:T(8,128)(2,1)S(1)} %copy.91), channel_id=2, replica_groups=mesh['row'=8,'col'=16] {'col'}, dimensions={0}, use_global_device_ids=true | all-gather | bytes 139264 | tf_op jit(solution)/shard_map/all_gather | solution.py:13
  33.9 13.7 %all_gather.10 = bf16[16,4,2048]{2,1,0:T(4,128)(2,1)S(1)} all-gather(bf16[16,4,256]{2,1,0:T(4,128)(2,1)} %param.16), channel_id=1, replica_groups=mesh['row'=8,'col'=16] {'row'}, dimensions={2}, use_global_device_ids=true | all-gather | bytes 294912 | tf_op jit(solution)/shard_map/all_gather | solution.py:88
  48.0 88.3 %while.11 = (s32[]{:T(128)}, f32[8,512,256]{2,1,0:T(8,128)}, s32[8]{0:T(128)S(1)}, s32[4096]{0:T(1024)S(1)}, bf16[16,4096]{1,0:T(8,128)(2,1)S(1)}, /*index=5*/bf...) while((s32[]{:T(128)}, f32[8,512,256]{2,1,0:T(8,128)}, ...), condition=%wide.region_3.4_spmd.clone, body=%wide.region_1.3_spmd.clone.sunk | while | flops 2315697664 | bytes 5122239 | solution.py:120
  50.8 8.3 %fusion.176 = f32[8,512,256]{2,1,0:T(8,128)} fusion(f32[8,512,256]{2,1,0:T(8,128)} %get-tuple-element.219, s32[]{:T(128)S(6)} %copy.99, bf16[8192,256]{1,0:T(8,128)(2,1)} %get-tuple-element.237, bf16[16,8192]{1,0:T(8,128)(2,1)S(1)} %get-tuple-element.235, f32[8192]{0:T(1024)S(1)} %get-tuple-element.236, f32[512]{0:T(512)S(1)} %multiply_reduce_fusion.13, ...), kind=kOutput, calls=%fused_computation.11.clone.1 | convolution fusion | flops 2315255808 | bytes 5066760 | tf_op jit(solution)/shard_map/while/body/eval_jaxpr/dot_general | solution.py:117
  61.8 8.3 %fusion.176 = f32[8,512,256]{2,1,0:T(8,128)} fusion(f32[8,512,256]{2,1,0:T(8,128)} %get-tuple-element.219, s32[]{:T(128)S(6)} %copy.99, bf16[8192,256]{1,0:T(8,128)(2,1)} %get-tuple-element.237, bf16[16,8192]{1,0:T(8,128)(2,1)S(1)} %get-tuple-element.235, f32[8192]{0:T(1024)S(1)} %get-tuple-element.236, f32[512]{0:T(512)S(1)} %multiply_reduce_fusion.13, ...), kind=kOutput, calls=%fused_computation.11.clone.1 | convolution fusion | flops 2315255808 | bytes 5066760 | tf_op jit(solution)/shard_map/while/body/eval_jaxpr/dot_general | solution.py:117
  72.8 8.3 %fusion.176 = f32[8,512,256]{2,1,0:T(8,128)} fusion(f32[8,512,256]{2,1,0:T(8,128)} %get-tuple-element.219, s32[]{:T(128)S(6)} %copy.99, bf16[8192,256]{1,0:T(8,128)(2,1)} %get-tuple-element.237, bf16[16,8192]{1,0:T(8,128)(2,1)S(1)} %get-tuple-element.235, f32[8192]{0:T(1024)S(1)} %get-tuple-element.236, f32[512]{0:T(512)S(1)} %multiply_reduce_fusion.13, ...), kind=kOutput, calls=%fused_computation.11.clone.1 | convolution fusion | flops 2315255808 | bytes 5066760 | tf_op jit(solution)/shard_map/while/body/eval_jaxpr/dot_general | solution.py:117
  83.9 8.3 %fusion.176 = f32[8,512,256]{2,1,0:T(8,128)} fusion(f32[8,512,256]{2,1,0:T(8,128)} %get-tuple-element.219, s32[]{:T(128)S(6)} %copy.99, bf16[8192,256]{1,0:T(8,128)(2,1)} %get-tuple-element.237, bf16[16,8192]{1,0:T(8,128)(2,1)S(1)} %get-tuple-element.235, f32[8192]{0:T(1024)S(1)} %get-tuple-element.236, f32[512]{0:T(512)S(1)} %multiply_reduce_fusion.13, ...), kind=kOutput, calls=%fused_computation.11.clone.1 | convolution fusion | flops 2315255808 | bytes 5066760 | tf_op jit(solution)/shard_map/while/body/eval_jaxpr/dot_general | solution.py:117
  94.9 8.3 %fusion.176 = f32[8,512,256]{2,1,0:T(8,128)} fusion(f32[8,512,256]{2,1,0:T(8,128)} %get-tuple-element.219, s32[]{:T(128)S(6)} %copy.99, bf16[8192,256]{1,0:T(8,128)(2,1)} %get-tuple-element.237, bf16[16,8192]{1,0:T(8,128)(2,1)S(1)} %get-tuple-element.235, f32[8192]{0:T(1024)S(1)} %get-tuple-element.236, f32[512]{0:T(512)S(1)} %multiply_reduce_fusion.13, ...), kind=kOutput, calls=%fused_computation.11.clone.1 | convolution fusion | flops 2315255808 | bytes 5066760 | tf_op jit(solution)/shard_map/while/body/eval_jaxpr/dot_general | solution.py:117
  106.0 8.3 %fusion.176 = f32[8,512,256]{2,1,0:T(8,128)} fusion(f32[8,512,256]{2,1,0:T(8,128)} %get-tuple-element.219, s32[]{:T(128)S(6)} %copy.99, bf16[8192,256]{1,0:T(8,128)(2,1)} %get-tuple-element.237, bf16[16,8192]{1,0:T(8,128)(2,1)S(1)} %get-tuple-element.235, f32[8192]{0:T(1024)S(1)} %get-tuple-element.236, f32[512]{0:T(512)S(1)} %multiply_reduce_fusion.13, ...), kind=kOutput, calls=%fused_computation.11.clone.1 | convolution fusion | flops 2315255808 | bytes 5066760 | tf_op jit(solution)/shard_map/while/body/eval_jaxpr/dot_general | solution.py:117
  117.0 8.3 %fusion.176 = f32[8,512,256]{2,1,0:T(8,128)} fusion(f32[8,512,256]{2,1,0:T(8,128)} %get-tuple-element.219, s32[]{:T(128)S(6)} %copy.99, bf16[8192,256]{1,0:T(8,128)(2,1)} %get-tuple-element.237, bf16[16,8192]{1,0:T(8,128)(2,1)S(1)} %get-tuple-element.235, f32[8192]{0:T(1024)S(1)} %get-tuple-element.236, f32[512]{0:T(512)S(1)} %multiply_reduce_fusion.13, ...), kind=kOutput, calls=%fused_computation.11.clone.1 | convolution fusion | flops 2315255808 | bytes 5066760 | tf_op jit(solution)/shard_map/while/body/eval_jaxpr/dot_general | solution.py:117
  128.0 8.3 %fusion.176 = f32[8,512,256]{2,1,0:T(8,128)} fusion(f32[8,512,256]{2,1,0:T(8,128)} %get-tuple-element.219, s32[]{:T(128)S(6)} %copy.99, bf16[8192,256]{1,0:T(8,128)(2,1)} %get-tuple-element.237, bf16[16,8192]{1,0:T(8,128)(2,1)S(1)} %get-tuple-element.235, f32[8192]{0:T(1024)S(1)} %get-tuple-element.236, f32[512]{0:T(512)S(1)} %multiply_reduce_fusion.13, ...), kind=kOutput, calls=%fused_computation.11.clone.1 | convolution fusion | flops 2315255808 | bytes 5066760 | tf_op jit(solution)/shard_map/while/body/eval_jaxpr/dot_general | solution.py:117
  144.2 2.8 collective-permute-start.4
  147.4 3.2 collective-permute-done.4
  150.7 88.6 %all-reduce.2.cloned.1.call-done = f32[4096,256]{1,0:T(8,128)} async-done(((f32[4096,256]{1,0:T(8,128)}), f32[4096,256]{1,0:T(8,128)}) %all-reduce.2.cloned.1.call-update) | async-done | bytes 4194320 | tf_op jit(solution)/shard_map/psum | solution.py:120
  242.7 11.7 %custom-call.18 = f32[2,64,64]{2,1,0:T(8,128)S(1)} custom-call(f32[2,64,64]{2,1,0:T(8,128)S(1)} %fusion.80), custom_call_target="Cholesky" | custom-call | tf_op jit(solution)/shard_map/vmap(jit(cholesky))/cholesky | solution.py:35
  254.6 9.8 %custom-call.19 = f32[2,1,64,64]{2,3,1,0:T(8,128)S(1)} custom-call(f32[2,1,64,64]{3,2,1,0:T(8,128)S(1)} %select_bitcast_fusion), custom_call_target="InvertDiagBlocksLowerTriangular" | custom-call | tf_op jit(solution)/shard_map/vmap(jit(_cho_solve))/triangular_solve | solution.py:37
  268.2 5.8 %cholesky.106 = f32[64,64]{1,0:T(8,128)S(1)} custom-call(f32[64,64]{1,0:T(8,128)S(1)} %fusion.101), custom_call_target="Cholesky" | custom-call | tf_op jit(solution)/shard_map/jit(cholesky)/cholesky | solution.py:35
  275.4 4.9 %custom-call.26 = f32[1,64,64]{1,2,0:T(8,128)S(1)} custom-call(f32[1,64,64]{2,1,0:T(8,128)S(1)} %fusion.84), custom_call_target="InvertDiagBlocksLowerTriangular" | custom-call | tf_op jit(solution)/shard_map/jit(_cho_solve)/triangular_solve | solution.py:37
  289.5 5.8 %cholesky.117 = f32[64,64]{1,0:T(8,128)S(1)} custom-call(f32[64,64]{1,0:T(8,128)S(1)} %fusion.96), custom_call_target="Cholesky" | custom-call | tf_op jit(solution)/shard_map/jit(cholesky)/cholesky | solution.py:35
  296.7 4.9 %custom-call.27 = f32[1,64,64]{1,2,0:T(8,128)S(1)} custom-call(f32[1,64,64]{2,1,0:T(8,128)S(1)} %fusion.85), custom_call_target="InvertDiagBlocksLowerTriangular" | custom-call | tf_op jit(solution)/shard_map/jit(_cho_solve)/triangular_solve | solution.py:37
  302.2 2.9 collective-permute-start.5
  308.3 3.1 collective-permute-done.3
  314.4 5.8 %cholesky.128 = f32[64,64]{1,0:T(8,128)S(1)} custom-call(f32[64,64]{1,0:T(8,128)S(1)} %fusion.91), custom_call_target="Cholesky" | custom-call | tf_op jit(solution)/shard_map/jit(cholesky)/cholesky | solution.py:35
  321.6 4.9 %custom-call.28 = f32[1,64,64]{1,2,0:T(8,128)S(1)} custom-call(f32[1,64,64]{2,1,0:T(8,128)S(1)} %fusion.86), custom_call_target="InvertDiagBlocksLowerTriangular" | custom-call | tf_op jit(solution)/shard_map/jit(_cho_solve)/triangular_solve | solution.py:37
  (161 shorter events, 43.5 us)
Async XLA Ops:
  7.2 40.8 %all-gather.3.cloned.1.call-start = ((), (), s32[]{:S(2)}) async-start(), calls=%async_computation | async-start | bytes 4718592 | tf_op jit(solution)/shard_map/all_gather | solution.py:84
  7.9 231.5 %all-reduce.2.cloned.1.call-start = ((), (), s32[]{:S(2)}) async-start(), calls=%async_computation.1 | async-start | bytes 8388608 | tf_op jit(solution)/shard_map/psum | solution.py:120
  136.3 0.7 copy-start.1
  136.3 2.3 copy-start.2
  139.4 4.0 %collective-permute-start.1 = (f32[16,64]{0,1:T(8,128)S(1)}, f32[16,64]{0,1:T(8,128)S(1)}, u32[]{:S(2)}, u32[]{:S(2)}) collective-permute-start(f32[16,64]{0,1:T(8,128)S(1)} %select_bitcast_fusion.3), channel_id=1, source_target_pairs={{0,1},{1,0},{2,3},{3,2},{4,5},{5,4},{6,7},{7,6},{8,9},{9,8},{10,11... | collective-permute-start | bytes 12296 | tf_op jit(solution)/shard_map/ppermute | solution.py:18
  144.2 6.4 %collective-permute-start.4 = (f32[16,64]{0,1:T(8,128)S(1)}, f32[16,64]{0,1:T(8,128)S(1)}, u32[]{:S(2)}, u32[]{:S(2)}) collective-permute-start(f32[16,64]{0,1:T(8,128)S(1)} %select_bitcast_fusion.2), channel_id=1, source_target_pairs={{0,2},{1,3},{2,0},{3,1},{4,6},{5,7},{6,4},{7,5},{8,10},{9,11},{10,... | collective-permute-start | bytes 12296 | tf_op jit(solution)/shard_map/ppermute | solution.py:18
  265.0 49.3 %copy-start = (f32[2,64,128]{2,1,0:T(8,128)}, f32[2,64,128]{2,1,0:T(8,128)S(1)}, u32[]{:S(2)}) copy-start(f32[2,64,128]{2,1,0:T(8,128)S(1)} %fusion.75) | copy-start | bytes 196612
  280.9 4.9 %collective-permute-start.2 = (f32[64,256]{1,0:T(8,128)S(1)}, f32[64,256]{1,0:T(8,128)S(1)}, u32[]{:S(2)}, u32[]{:S(2)}) collective-permute-start(f32[64,256]{1,0:T(8,128)S(1)} %fusion.64), channel_id=1, source_target_pairs={{0,1},{1,0},{2,3},{3,2},{4,5},{5,4},{6,7},{7,6},{8,9},{9,8},{10,11... | collective-permute-start | bytes 196616 | tf_op jit(solution)/shard_map/ppermute | solution.py:18
  282.4 4.3 %collective-permute-start = (f32[64,256]{1,0:T(8,128)S(1)}, f32[64,256]{1,0:T(8,128)S(1)}, u32[]{:S(2)}, u32[]{:S(2)}) collective-permute-start(f32[64,256]{1,0:T(8,128)S(1)} %get-tuple-element.116), channel_id=1, source_target_pairs={{0,1},{1,0},{2,3},{3,2},{4,5},{5,4},{6,7},{7,6},{8,9},{9,8},{10,11... | collective-permute-start | bytes 196616 | tf_op jit(solution)/shard_map/ppermute | solution.py:18
  302.2 5.8 %collective-permute-start.5 = (f32[64,256]{1,0:T(8,128)S(1)}, f32[64,256]{1,0:T(8,128)S(1)}, u32[]{:S(2)}, u32[]{:S(2)}) collective-permute-start(f32[64,256]{1,0:T(8,128)S(1)} %fusion.68), channel_id=1, source_target_pairs={{0,2},{1,3},{2,0},{3,1},{4,6},{5,7},{6,4},{7,5},{8,10},{9,11},{10,... | collective-permute-start | bytes 196616 | tf_op jit(solution)/shard_map/ppermute | solution.py:18
  305.4 6.1 %collective-permute-start.3 = (f32[64,256]{1,0:T(8,128)S(1)}, f32[64,256]{1,0:T(8,128)S(1)}, u32[]{:S(2)}, u32[]{:S(2)}) collective-permute-start(f32[64,256]{1,0:T(8,128)S(1)} %get-tuple-element.114), channel_id=1, source_target_pairs={{0,2},{1,3},{2,0},{3,1},{4,6},{5,7},{6,4},{7,5},{8,10},{9,11},{10,... | collective-permute-start | bytes 196616 | tf_op jit(solution)/shard_map/ppermute | solution.py:18
Sparse Core Ops, SparseCore 0:
  9.7 35.7 all-gather.2
  136.5 102.8 all-reduce.1
